TPU v7x, 512 devices: a whole 4x8x8 slice. The times are simulated.
512 devices in a mesh: probe: 8 (over y_lo, core), space: 64 (over y_hi, x, z).
Axes of the slice: x: 4, y: 8 (y_hi: 2, y_lo: 4; y = y_hi * 4 + y_lo), z: 8, core: 2. Of those that a mesh axis runs over, the one named last changes fastest.
Arguments:
- probe_dirs: float32 [32, 64, 256], P('probe', 'space'), may hold values from -6 to 6
- log_param: float32 [64, 256], P('space'), may hold values from -1 to 1
- background: float32 [512, 32, 512], P('space'), may hold values from 0.3 to 1.5
- site_class: int32 [512, 32, 512], P('space'), may hold values from 0 to 3
- trap_density: float32 [4], replicated, may hold values from 0.2 to 1
Outputs:
- q_basis: float32 [32, 64, 256], P('probe', 'space')
- lower_factor: float32 [32, 32], replicated
All inputs are finite; a program needn't handle non-finite values.
Results may differ from a plain program's by a relative error of at most 0.0003.
Values sent between devices are 32-bit elements; how exact they have to be, the bound alone decides.
A program may use at most 64 MiB of HBM per device.

v0:
```python
import jax
import jax.numpy as jnp
from jax import lax
from jax.sharding import PartitionSpec as P

PX = 64
PY = 4
REF = 8
STEPS = 4
TIME_STEP = 0.12


def padded_2(x, sides, width):
    for axis, dim in sides:
        count, length = (lax.axis_size(axis), x.shape[dim])
        up = [(i, (i + 1) % count) for i in range(count - 1)]
        down = [(j, i) for i, j in up]
        last = lax.slice_in_dim(x, length - width, length, axis=dim)
        first = lax.slice_in_dim(x, 0, width, axis=dim)
        before = lax.ppermute(last, axis, up)
        after = lax.ppermute(first, axis, down)
        x = jnp.concatenate([before, x, after], axis=dim)
    return x


def lower_solve(factor, rows):
    return lax.linalg.triangular_solve(factor, rows, left_side=True, lower=True)


def prolong(coarse):
    leading = coarse.shape[:-2]
    planes = coarse.shape[-2]
    coarse_grid = coarse.reshape(leading + (planes, PY, PX))
    expanded = jnp.broadcast_to(
        coarse_grid[..., :, None, :, None, :, None], leading + (planes, REF, PY, REF, PX, REF)
    )
    return expanded.reshape(leading + (planes * REF, PY * REF, PX * REF))


def restrict(finegrid):
    probe_count = finegrid.shape[0]
    planes = finegrid.shape[1] // REF
    shaped = finegrid.reshape((probe_count, planes, REF, PY, REF, PX, REF))
    return jnp.sum(shaped, axis=(2, 4, 6)).reshape((probe_count, planes, PY * PX))


def stencil(padded, current, trap_rate):
    up_down = padded[:, 2:, :, :] + padded[:, :-2, :, :]
    flat_pad = jnp.pad(current, ((0, 0), (0, 0), (1, 1), (1, 1)))
    lateral = (
        flat_pad[:, :, 2:, 1:-1]
        + flat_pad[:, :, :-2, 1:-1]
        + flat_pad[:, :, 1:-1, 2:]
        + flat_pad[:, :, 1:-1, :-2]
    )
    return current + TIME_STEP * (up_down + lateral - 6.0 * current - trap_rate[None] * current)


def cholesky_pass(rows, gram_sum, cell_count):
    highest = lax.Precision.HIGHEST
    partial_gram = jnp.dot(rows, rows.T, precision=highest, preferred_element_type=jnp.float32)
    gram_matrix = gram_sum(partial_gram) / cell_count
    factor = jnp.linalg.cholesky(gram_matrix)
    return (lower_solve(factor, rows), factor)


def shards(probe_dirs, log_param, background, site_class, trap_density):
    probe_count = probe_dirs.shape[0]
    planes = probe_dirs.shape[1]
    plane_cells = probe_dirs.shape[2]
    density = jnp.zeros(site_class.shape, jnp.float32)
    for class_index in range(trap_density.shape[0]):
        density = density + jnp.where(site_class == class_index, trap_density[class_index], 0.0)
    trap_rate = density * jnp.exp(prolong(log_param))
    source = -TIME_STEP * trap_rate * background
    tangent = source[None] * prolong(probe_dirs)
    for step_index in range(STEPS - 1):
        padded = padded_2(tangent, (("space", 1),), 1)
        tangent = stencil(padded, tangent, trap_rate)
    adjoint = tangent
    summed = adjoint
    for step_index in range(STEPS - 1):
        padded = padded_2(adjoint, (("space", 1),), 1)
        adjoint = stencil(padded, adjoint, trap_rate)
        summed = summed + adjoint
    images = restrict(source[None] * summed).reshape((probe_count, planes * plane_cells))
    cell_count = float(planes * lax.axis_size("space") * plane_cells)
    highest = lax.Precision.HIGHEST
    every_probe = lax.all_gather(images, "probe", axis=0, tiled=True)

    def space_sum(partial_gram):
        return lax.psum(partial_gram, "space")

    basis_one, factor_one = cholesky_pass(every_probe, space_sum, cell_count)
    q_rows, factor_two = cholesky_pass(basis_one, space_sum, cell_count)
    q_local = lax.dynamic_slice_in_dim(
        q_rows, lax.axis_index("probe") * probe_count, probe_count, 0
    )
    lower_factor = jnp.dot(
        factor_one, factor_two, precision=highest, preferred_element_type=jnp.float32
    )
    return (q_local.reshape((probe_count, planes, plane_cells)), lower_factor)


def solution(mesh):
    placed = (
        P("probe", "space", None),
        P("space", None),
        P("space", None, None),
        P("space", None, None),
        P(),
    )
    return jax.shard_map(
        shards,
        mesh=mesh,
        in_specs=placed,
        out_specs=(P("probe", "space", None), P()),
        check_vma=False,
    )
```

profile of v0, /device:TPU:56, one launch (start us, length us, event | category | flops | bytes accessed | tf_op | source)
XLA Modules:
  0.0 1067.1 jit_solution(6931667937898231620)
XLA Ops:
  6.2 4.1 broadcast_in_dim.56
  10.3 2.8 multiply_multiply_fusion.2
  13.4 15.4 %collective-permute-start = (f32[4,1,32,512]{3,2,1,0:T(8,128)S(1)}, f32[4,1,32,512]{3,2,1,0:T(8,128)S(1)}, u32[]{:S(2)}, u32[]{:S(2)}) collective-permute-start(f32[4,1,32,512]{3,2,1,0:T(8,128)S(1)} %get-tuple-element.16), channel_id=1, source_target_pairs={{1,0},{2,1},{3,2},{4,3},{5,4},{6,5},{7,6},{8,7},{9,8},{10,9},{11,1... | collective-permute-start | bytes 786440 | tf_op jit(solution)/shard_map/ppermute | solution.py:21
  30.7 3.6 collective-permute-done
  34.3 12.3 %collective-permute-done.1 = f32[4,1,32,512]{3,2,1,0:T(8,128)S(1)} collective-permute-done((f32[4,1,32,512]{3,2,1,0:T(8,128)S(1)}, f32[4,1,32,512]{3,2,1,0:T(8,128)S(1)}, u32[]{:S(2)}, u32[]{:S(2)}) %collective-permute-start.1) | collective-permute-done | bytes 262176 | tf_op jit(solution)/shard_map/ppermute | solution.py:20
  51.0 3.9 collective-permute-start.3
  54.9 2.8 collective-permute-done.2
  57.8 10.2 collective-permute-done.3
  72.4 3.9 collective-permute-start.5
  78.7 10.1 collective-permute-done.5
  93.2 3.9 collective-permute-start.7
  99.6 10.1 collective-permute-done.7
  114.0 3.9 collective-permute-start.9
  120.3 10.1 collective-permute-done.9
  137.0 4.1 collective-permute-start.11
  143.6 10.1 collective-permute-done.11
  153.8 10.9 %fusion.55 = f32[4,32,512]{2,1,0:T(8,128)} fusion(f32[4,8,32,512]{3,2,1,0:T(8,128)} %copy-done, f32[4,1,32,512]{3,2,1,0:T(8,128)} %collective-permute-done.11, f32[4,1,32,512]{3,2,1,0:T(8,128)} %collective-permute-done.10, f32[4,8,32,512]{3,2,1,0:T(8,128)S(1)} %fusion.22, f32[8,32,512]{2,1,0:T(8,128)S(1)} %get-tuple-element.5, ...), kind=kLoop, calls=%fused_computation.94 | loop fusion | flops 16187392 | bytes 6553600 | tf_op jit(solution)/shard_map/reduce_sum | solution.py:44
  164.7 4.5 reduce_sum.14
  169.2 2.6 reduce_sum.18
  171.8 22.3 %all-gather = f32[8,4,256]{2,1,0:T(4,128)S(1)} all-gather(f32[1,4,256]{2,1,0:T(4,128)S(1)} %reshape.39), channel_id=1, replica_groups=mesh['probe'=8,'space'=64] {'probe'}, dimensions={0}, use_global_device_ids=true | all-gather | bytes 36864 | tf_op jit(solution)/shard_map/all_gather | solution.py:89
  194.3 427.9 %psum.14 = f32[32,32]{0,1:T(8,128)S(1)} all-reduce(f32[32,32]{0,1:T(8,128)S(1)} %fusion.84), channel_id=1, replica_groups=mesh['probe'=8,'space'=64] {'space'}, use_global_device_ids=true, to_apply=%region_2.3 | all-reduce | flops 1024 | bytes 8192 | tf_op jit(solution)/shard_map/psum | solution.py:92
  622.2 2.9 cholesky.44
  629.3 427.9 %psum.15 = f32[32,32]{0,1:T(8,128)S(1)} all-reduce(f32[32,32]{0,1:T(8,128)S(1)} %fusion.85), channel_id=1, replica_groups=mesh['probe'=8,'space'=64] {'space'}, use_global_device_ids=true, to_apply=%region_5.8 | all-reduce | flops 1024 | bytes 8192 | tf_op jit(solution)/shard_map/psum | solution.py:92
  1057.3 2.9 cholesky.55
  (63 shorter events, 53.0 us)
Async XLA Ops:
  0.6 2.9 copy-start.4
  6.2 4.1 copy-start.2
  6.2 4.1 copy-start.3
  13.4 20.9 %collective-permute-start = (f32[4,1,32,512]{3,2,1,0:T(8,128)S(1)}, f32[4,1,32,512]{3,2,1,0:T(8,128)S(1)}, u32[]{:S(2)}, u32[]{:S(2)}) collective-permute-start(f32[4,1,32,512]{3,2,1,0:T(8,128)S(1)} %get-tuple-element.16), channel_id=1, source_target_pairs={{1,0},{2,1},{3,2},{4,3},{5,4},{6,5},{7,6},{8,7},{9,8},{10,9},{11,1... | collective-permute-start | bytes 786440 | tf_op jit(solution)/shard_map/ppermute | solution.py:21
  28.8 17.9 %collective-permute-start.1 = (f32[4,1,32,512]{3,2,1,0:T(8,128)S(1)}, f32[4,1,32,512]{3,2,1,0:T(8,128)S(1)}, u32[]{:S(2)}, u32[]{:S(2)}) collective-permute-start(f32[4,1,32,512]{3,2,1,0:T(8,128)S(1)} %get-tuple-element.17), channel_id=1, source_target_pairs={{0,1},{1,2},{2,3},{3,4},{4,5},{5,6},{6,7},{7,8},{8,9},{9,10},{10,1... | collective-permute-start | bytes 786440 | tf_op jit(solution)/shard_map/ppermute | solution.py:20
  49.1 8.7 collective-permute-start.2
  51.0 16.9 %collective-permute-start.3 = (f32[4,1,32,512]{3,2,1,0:T(8,128)S(1)}, f32[4,1,32,512]{3,2,1,0:T(8,128)S(1)}, u32[]{:S(2)}, u32[]{:S(2)}) collective-permute-start(f32[4,1,32,512]{3,2,1,0:T(8,128)S(1)} %get-tuple-element.15), channel_id=1, source_target_pairs={{0,1},{1,2},{2,3},{3,4},{4,5},{5,6},{6,7},{7,8},{8,9},{9,10},{10,1... | collective-permute-start | bytes 786440 | tf_op jit(solution)/shard_map/ppermute | solution.py:20
  70.4 8.3 collective-permute-start.4
  72.4 16.4 %collective-permute-start.5 = (f32[4,1,32,512]{3,2,1,0:T(8,128)S(1)}, f32[4,1,32,512]{3,2,1,0:T(8,128)S(1)}, u32[]{:S(2)}, u32[]{:S(2)}) collective-permute-start(f32[4,1,32,512]{3,2,1,0:T(8,128)S(1)} %get-tuple-element.13), channel_id=1, source_target_pairs={{0,1},{1,2},{2,3},{3,4},{4,5},{5,6},{6,7},{7,8},{8,9},{9,10},{10,1... | collective-permute-start | bytes 786440 | tf_op jit(solution)/shard_map/ppermute | solution.py:20
  91.3 8.3 collective-permute-start.6
  93.2 16.4 %collective-permute-start.7 = (f32[4,1,32,512]{3,2,1,0:T(8,128)S(1)}, f32[4,1,32,512]{3,2,1,0:T(8,128)S(1)}, u32[]{:S(2)}, u32[]{:S(2)}) collective-permute-start(f32[4,1,32,512]{3,2,1,0:T(8,128)S(1)} %get-tuple-element.11), channel_id=1, source_target_pairs={{0,1},{1,2},{2,3},{3,4},{4,5},{5,6},{6,7},{7,8},{8,9},{9,10},{10,1... | collective-permute-start | bytes 786440 | tf_op jit(solution)/shard_map/ppermute | solution.py:20
  109.6 2.4 copy-start.1
  112.0 8.3 collective-permute-start.8
  114.0 16.4 %collective-permute-start.9 = (f32[4,1,32,512]{3,2,1,0:T(8,128)S(1)}, f32[4,1,32,512]{3,2,1,0:T(8,128)S(1)}, u32[]{:S(2)}, u32[]{:S(2)}) collective-permute-start(f32[4,1,32,512]{3,2,1,0:T(8,128)S(1)} %get-tuple-element.9), channel_id=1, source_target_pairs={{0,1},{1,2},{2,3},{3,4},{4,5},{5,6},{6,7},{7,8},{8,9},{9,10},{10,1... | collective-permute-start | bytes 786440 | tf_op jit(solution)/shard_map/ppermute | solution.py:20
  132.8 1.4 copy-start
  135.0 8.6 collective-permute-start.10
  137.0 16.8 %collective-permute-start.11 = (f32[4,1,32,512]{3,2,1,0:T(8,128)}, f32[4,1,32,512]{3,2,1,0:T(8,128)}, u32[]{:S(2)}, u32[]{:S(2)}) collective-permute-start(f32[4,1,32,512]{3,2,1,0:T(8,128)} %get-tuple-element.7), channel_id=1, source_target_pairs={{0,1},{1,2},{2,3},{3,4},{4,5},{5,6},{6,7},{7,8},{8,9},{9,10},{10,1... | collective-permute-start | bytes 786440 | tf_op jit(solution)/shard_map/ppermute | solution.py:20
where the time goes:
time: 1070 us
  blocking collectives  878 us (82%)
  waiting for transfers between devices  79 us (7%)
  starting transfers between devices  46.7 us (4%)
  other arithmetic  42.2 us (4%)
  local copies, waits for them, and re-layouts  17.3 us (2%)
    psum x2, blocking collectives, space_sum(): return lax.psum(partial_gram, 'space')  856 us
    ppermute x6, waiting for transfers between devices, padded_2(): before = lax.ppermute(last, axis, up)  62.8 us
    ppermute x6, starting transfers between devices, padded_2(): after = lax.ppermute(first, axis, down)  25 us
    all_gather x1, blocking collectives, shards(): every_probe = lax.all_gather(images, 'probe', axis=0, tiled=True)  22.3 us
    ppermute x6, starting transfers between devices, padded_2(): before = lax.ppermute(last, axis, up)  21.7 us
  transfers between devices with their start and end apart: 12, of which 12 were waited for; matrix products, arithmetic and copies ran while one was open for 0% of the time, Pallas kernels for 0%

commit v1 on v0

--- a/solution.py
+++ b/solution.py
@@ -8,6 +8,11 @@
 REF = 8
 STEPS = 4
 TIME_STEP = 0.12
+
+
+def rates_refer(t0):
+    k_now = lax.all_gather(t0, "space").sum(axis=0)
+    return k_now
 
 
 def padded_2(x, sides, width):
@@ -89,7 +94,7 @@
     every_probe = lax.all_gather(images, "probe", axis=0, tiled=True)
 
     def space_sum(partial_gram):
-        return lax.psum(partial_gram, "space")
+        return rates_refer(partial_gram)
 
     basis_one, factor_one = cholesky_pass(every_probe, space_sum, cell_count)
     q_rows, factor_two = cholesky_pass(basis_one, space_sum, cell_count)

time: 1070 us -> 652 us (0.61)
  blocking collectives: 878 us -> 461 us
    psum x2 -> x0, blocking collectives: 856 us -> none  [space_sum(): return lax.psum(partial_gram, 'space')]
    all_gather x0 -> x2, blocking collectives: none -> 439 us  [rates_refer(): k_now = lax.all_gather(t0, 'space').sum(axis=0)]
where the time goes in v1:
time: 652 us; the launch traced here: 651 us
  blocking collectives  461 us (71%)
  waiting for transfers between devices  79.1 us (12%)
  starting transfers between devices  46.7 us (7%)
  other arithmetic  42.5 us (7%)
  local copies, waits for them, and re-layouts  17.5 us (3%)
    all_gather x2, blocking collectives, rates_refer(): k_now = lax.all_gather(t0, 'space').sum(axis=0)  439 us
    ppermute x6, waiting for transfers between devices, padded_2(): before = lax.ppermute(last, axis, up)  62.9 us
    ppermute x6, starting transfers between devices, padded_2(): after = lax.ppermute(first, axis, down)  25 us
    all_gather x1, blocking collectives, shards(): every_probe = lax.all_gather(images, 'probe', axis=0, tiled=True)  22.1 us
    ppermute x6, starting transfers between devices, padded_2(): before = lax.ppermute(last, axis, up)  21.7 us
    ppermute x6, waiting for transfers between devices, padded_2(): after = lax.ppermute(first, axis, down)  16.2 us
    reduce_sum x2, other arithmetic, restrict(): jnp.sum(shaped, axis=(2, 4, 6)).reshape((probe_count, planes, PY * PX))  13.5 us
  transfers between devices with their start and end apart: 12, of which 12 were waited for; matrix products, arithmetic and copies ran while one was open for 0% of the time, Pallas kernels for 0%

profile of v1, /device:TPU:56, one launch (start us, length us, event | category | flops | bytes accessed | tf_op | source)
XLA Modules:
  0.0 651.0 jit_solution(11453515356108447419)
XLA Ops:
  6.2 4.1 broadcast_in_dim.56
  10.3 2.8 multiply_multiply_fusion.2
  13.3 15.4 %collective-permute-start = (f32[4,1,32,512]{3,2,1,0:T(8,128)S(1)}, f32[4,1,32,512]{3,2,1,0:T(8,128)S(1)}, u32[]{:S(2)}, u32[]{:S(2)}) collective-permute-start(f32[4,1,32,512]{3,2,1,0:T(8,128)S(1)} %get-tuple-element.16), channel_id=1, source_target_pairs={{1,0},{2,1},{3,2},{4,3},{5,4},{6,5},{7,6},{8,7},{9,8},{10,9},{11,1... | collective-permute-start | bytes 786440 | tf_op jit(solution)/shard_map/ppermute | solution.py:26
  30.7 3.6 collective-permute-done
  34.3 12.3 %collective-permute-done.1 = f32[4,1,32,512]{3,2,1,0:T(8,128)S(1)} collective-permute-done((f32[4,1,32,512]{3,2,1,0:T(8,128)S(1)}, f32[4,1,32,512]{3,2,1,0:T(8,128)S(1)}, u32[]{:S(2)}, u32[]{:S(2)}) %collective-permute-start.1) | collective-permute-done | bytes 262176 | tf_op jit(solution)/shard_map/ppermute | solution.py:25
  51.0 3.9 collective-permute-start.3
  55.0 2.8 collective-permute-done.2
  57.8 10.2 %collective-permute-done.3 = f32[4,1,32,512]{3,2,1,0:T(8,128)S(1)} collective-permute-done((f32[4,1,32,512]{3,2,1,0:T(8,128)S(1)}, f32[4,1,32,512]{3,2,1,0:T(8,128)S(1)}, u32[]{:S(2)}, u32[]{:S(2)}) %collective-permute-start.3) | collective-permute-done | bytes 262176 | tf_op jit(solution)/shard_map/ppermute | solution.py:25
  72.4 3.9 collective-permute-start.5
  78.8 10.1 %collective-permute-done.5 = f32[4,1,32,512]{3,2,1,0:T(8,128)S(1)} collective-permute-done((f32[4,1,32,512]{3,2,1,0:T(8,128)S(1)}, f32[4,1,32,512]{3,2,1,0:T(8,128)S(1)}, u32[]{:S(2)}, u32[]{:S(2)}) %collective-permute-start.5) | collective-permute-done | bytes 262176 | tf_op jit(solution)/shard_map/ppermute | solution.py:25
  93.3 3.9 collective-permute-start.7
  99.6 10.1 %collective-permute-done.7 = f32[4,1,32,512]{3,2,1,0:T(8,128)S(1)} collective-permute-done((f32[4,1,32,512]{3,2,1,0:T(8,128)S(1)}, f32[4,1,32,512]{3,2,1,0:T(8,128)S(1)}, u32[]{:S(2)}, u32[]{:S(2)}) %collective-permute-start.7) | collective-permute-done | bytes 262176 | tf_op jit(solution)/shard_map/ppermute | solution.py:25
  114.0 3.9 collective-permute-start.9
  120.4 10.1 %collective-permute-done.9 = f32[4,1,32,512]{3,2,1,0:T(8,128)S(1)} collective-permute-done((f32[4,1,32,512]{3,2,1,0:T(8,128)S(1)}, f32[4,1,32,512]{3,2,1,0:T(8,128)S(1)}, u32[]{:S(2)}, u32[]{:S(2)}) %collective-permute-start.9) | collective-permute-done | bytes 262176 | tf_op jit(solution)/shard_map/ppermute | solution.py:25
  137.0 4.1 collective-permute-start.11
  143.7 10.2 %collective-permute-done.11 = f32[4,1,32,512]{3,2,1,0:T(8,128)} collective-permute-done((f32[4,1,32,512]{3,2,1,0:T(8,128)}, f32[4,1,32,512]{3,2,1,0:T(8,128)}, u32[]{:S(2)}, u32[]{:S(2)}) %collective-permute-start.11) | collective-permute-done | bytes 262176 | tf_op jit(solution)/shard_map/ppermute | solution.py:25
  153.9 10.9 %fusion.55 = f32[4,32,512]{2,1,0:T(8,128)} fusion(f32[4,8,32,512]{3,2,1,0:T(8,128)} %copy-done, f32[4,1,32,512]{3,2,1,0:T(8,128)} %collective-permute-done.11, f32[4,1,32,512]{3,2,1,0:T(8,128)} %collective-permute-done.10, f32[4,8,32,512]{3,2,1,0:T(8,128)S(1)} %fusion.22, f32[8,32,512]{2,1,0:T(8,128)S(1)} %get-tuple-element.5, ...), kind=kLoop, calls=%fused_computation.94 | loop fusion | flops 16187392 | bytes 6553600 | tf_op jit(solution)/shard_map/reduce_sum | solution.py:49
  164.8 4.5 reduce_sum.35
  169.3 2.6 reduce_sum.36
  172.0 22.1 %all-gather.2 = f32[8,4,256]{2,1,0:T(4,128)S(1)} all-gather(f32[1,4,256]{2,1,0:T(4,128)S(1)} %reshape.41), channel_id=1, replica_groups=mesh['probe'=8,'space'=64] {'probe'}, dimensions={0}, use_global_device_ids=true | all-gather | bytes 36864 | tf_op jit(solution)/shard_map/all_gather | solution.py:94
  194.3 218.6 %all-gather = f32[2048,32]{1,0:T(8,128)S(1)} all-gather(f32[32,32]{1,0:T(8,128)S(1)} %fusion.84), channel_id=2, replica_groups=mesh['probe'=8,'space'=64] {'space'}, dimensions={0}, use_global_device_ids=true | all-gather | bytes 266240 | tf_op jit(solution)/shard_map/all_gather | solution.py:14
  413.1 2.9 cholesky.44
  420.3 220.7 %all-gather.1 = f32[2048,32]{1,0:T(8,128)S(1)} all-gather(f32[32,32]{1,0:T(8,128)S(1)} %fusion.85), channel_id=3, replica_groups=mesh['probe'=8,'space'=64] {'space'}, dimensions={0}, use_global_device_ids=true | all-gather | bytes 266240 | tf_op jit(solution)/shard_map/all_gather | solution.py:14
  641.2 2.9 cholesky.55
  (67 shorter events, 53.5 us)
Async XLA Ops:
  0.6 2.9 copy-start.4
  6.2 4.1 copy-start.2
  6.2 4.1 copy-start.3
  13.3 20.9 %collective-permute-start = (f32[4,1,32,512]{3,2,1,0:T(8,128)S(1)}, f32[4,1,32,512]{3,2,1,0:T(8,128)S(1)}, u32[]{:S(2)}, u32[]{:S(2)}) collective-permute-start(f32[4,1,32,512]{3,2,1,0:T(8,128)S(1)} %get-tuple-element.16), channel_id=1, source_target_pairs={{1,0},{2,1},{3,2},{4,3},{5,4},{6,5},{7,6},{8,7},{9,8},{10,9},{11,1... | collective-permute-start | bytes 786440 | tf_op jit(solution)/shard_map/ppermute | solution.py:26
  28.7 17.9 %collective-permute-start.1 = (f32[4,1,32,512]{3,2,1,0:T(8,128)S(1)}, f32[4,1,32,512]{3,2,1,0:T(8,128)S(1)}, u32[]{:S(2)}, u32[]{:S(2)}) collective-permute-start(f32[4,1,32,512]{3,2,1,0:T(8,128)S(1)} %get-tuple-element.17), channel_id=1, source_target_pairs={{0,1},{1,2},{2,3},{3,4},{4,5},{5,6},{6,7},{7,8},{8,9},{9,10},{10,1... | collective-permute-start | bytes 786440 | tf_op jit(solution)/shard_map/ppermute | solution.py:25
  49.1 8.7 %collective-permute-start.2 = (f32[4,1,32,512]{3,2,1,0:T(8,128)S(1)}, f32[4,1,32,512]{3,2,1,0:T(8,128)S(1)}, u32[]{:S(2)}, u32[]{:S(2)}) collective-permute-start(f32[4,1,32,512]{3,2,1,0:T(8,128)S(1)} %get-tuple-element.14), channel_id=1, source_target_pairs={{1,0},{2,1},{3,2},{4,3},{5,4},{6,5},{7,6},{8,7},{9,8},{10,9},{11,1... | collective-permute-start | bytes 786440 | tf_op jit(solution)/shard_map/ppermute | solution.py:26
  51.0 16.9 %collective-permute-start.3 = (f32[4,1,32,512]{3,2,1,0:T(8,128)S(1)}, f32[4,1,32,512]{3,2,1,0:T(8,128)S(1)}, u32[]{:S(2)}, u32[]{:S(2)}) collective-permute-start(f32[4,1,32,512]{3,2,1,0:T(8,128)S(1)} %get-tuple-element.15), channel_id=1, source_target_pairs={{0,1},{1,2},{2,3},{3,4},{4,5},{5,6},{6,7},{7,8},{8,9},{9,10},{10,1... | collective-permute-start | bytes 786440 | tf_op jit(solution)/shard_map/ppermute | solution.py:25
  70.5 8.3 %collective-permute-start.4 = (f32[4,1,32,512]{3,2,1,0:T(8,128)S(1)}, f32[4,1,32,512]{3,2,1,0:T(8,128)S(1)}, u32[]{:S(2)}, u32[]{:S(2)}) collective-permute-start(f32[4,1,32,512]{3,2,1,0:T(8,128)S(1)} %get-tuple-element.12), channel_id=1, source_target_pairs={{1,0},{2,1},{3,2},{4,3},{5,4},{6,5},{7,6},{8,7},{9,8},{10,9},{11,1... | collective-permute-start | bytes 786440 | tf_op jit(solution)/shard_map/ppermute | solution.py:26
  72.4 16.4 %collective-permute-start.5 = (f32[4,1,32,512]{3,2,1,0:T(8,128)S(1)}, f32[4,1,32,512]{3,2,1,0:T(8,128)S(1)}, u32[]{:S(2)}, u32[]{:S(2)}) collective-permute-start(f32[4,1,32,512]{3,2,1,0:T(8,128)S(1)} %get-tuple-element.13), channel_id=1, source_target_pairs={{0,1},{1,2},{2,3},{3,4},{4,5},{5,6},{6,7},{7,8},{8,9},{9,10},{10,1... | collective-permute-start | bytes 786440 | tf_op jit(solution)/shard_map/ppermute | solution.py:25
  91.4 8.3 %collective-permute-start.6 = (f32[4,1,32,512]{3,2,1,0:T(8,128)S(1)}, f32[4,1,32,512]{3,2,1,0:T(8,128)S(1)}, u32[]{:S(2)}, u32[]{:S(2)}) collective-permute-start(f32[4,1,32,512]{3,2,1,0:T(8,128)S(1)} %get-tuple-element.10), channel_id=1, source_target_pairs={{1,0},{2,1},{3,2},{4,3},{5,4},{6,5},{7,6},{8,7},{9,8},{10,9},{11,1... | collective-permute-start | bytes 786440 | tf_op jit(solution)/shard_map/ppermute | solution.py:26
  93.3 16.4 %collective-permute-start.7 = (f32[4,1,32,512]{3,2,1,0:T(8,128)S(1)}, f32[4,1,32,512]{3,2,1,0:T(8,128)S(1)}, u32[]{:S(2)}, u32[]{:S(2)}) collective-permute-start(f32[4,1,32,512]{3,2,1,0:T(8,128)S(1)} %get-tuple-element.11), channel_id=1, source_target_pairs={{0,1},{1,2},{2,3},{3,4},{4,5},{5,6},{6,7},{7,8},{8,9},{9,10},{10,1... | collective-permute-start | bytes 786440 | tf_op jit(solution)/shard_map/ppermute | solution.py:25
  109.7 2.4 copy-start.1
  112.1 8.3 %collective-permute-start.8 = (f32[4,1,32,512]{3,2,1,0:T(8,128)S(1)}, f32[4,1,32,512]{3,2,1,0:T(8,128)S(1)}, u32[]{:S(2)}, u32[]{:S(2)}) collective-permute-start(f32[4,1,32,512]{3,2,1,0:T(8,128)S(1)} %get-tuple-element.8), channel_id=1, source_target_pairs={{1,0},{2,1},{3,2},{4,3},{5,4},{6,5},{7,6},{8,7},{9,8},{10,9},{11,1... | collective-permute-start | bytes 786440 | tf_op jit(solution)/shard_map/ppermute | solution.py:26
  114.0 16.4 %collective-permute-start.9 = (f32[4,1,32,512]{3,2,1,0:T(8,128)S(1)}, f32[4,1,32,512]{3,2,1,0:T(8,128)S(1)}, u32[]{:S(2)}, u32[]{:S(2)}) collective-permute-start(f32[4,1,32,512]{3,2,1,0:T(8,128)S(1)} %get-tuple-element.9), channel_id=1, source_target_pairs={{0,1},{1,2},{2,3},{3,4},{4,5},{5,6},{6,7},{7,8},{8,9},{9,10},{10,1... | collective-permute-start | bytes 786440 | tf_op jit(solution)/shard_map/ppermute | solution.py:25
  132.9 1.4 copy-start
  135.1 8.6 %collective-permute-start.10 = (f32[4,1,32,512]{3,2,1,0:T(8,128)}, f32[4,1,32,512]{3,2,1,0:T(8,128)}, u32[]{:S(2)}, u32[]{:S(2)}) collective-permute-start(f32[4,1,32,512]{3,2,1,0:T(8,128)} %get-tuple-element.6), channel_id=1, source_target_pairs={{1,0},{2,1},{3,2},{4,3},{5,4},{6,5},{7,6},{8,7},{9,8},{10,9},{11,1... | collective-permute-start | bytes 786440 | tf_op jit(solution)/shard_map/ppermute | solution.py:26
  137.0 16.9 %collective-permute-start.11 = (f32[4,1,32,512]{3,2,1,0:T(8,128)}, f32[4,1,32,512]{3,2,1,0:T(8,128)}, u32[]{:S(2)}, u32[]{:S(2)}) collective-permute-start(f32[4,1,32,512]{3,2,1,0:T(8,128)} %get-tuple-element.7), channel_id=1, source_target_pairs={{0,1},{1,2},{2,3},{3,4},{4,5},{5,6},{6,7},{7,8},{8,9},{9,10},{10,1... | collective-permute-start | bytes 786440 | tf_op jit(solution)/shard_map/ppermute | solution.py:25
